TPU v7x, 128 devices: a whole 4x4x4 slice. The times are simulated.
128 devices in a mesh: band: 8 (over z_hi, x), slab: 16 (over z_lo, y, core).
Axes of the slice: x: 4, y: 4, z: 4 (z_hi: 2, z_lo: 2; z = z_hi * 2 + z_lo), core: 2. Of those that a mesh axis runs over, the one named last changes fastest.
Arguments:
- orbitals: bfloat16 [32, 256, 256, 256], P('band', 'slab'), may hold values from -6 to 6
- occupation: float32 [32], P('band'), may hold values from 0.2 to 2
Outputs:
- density: float32 [256, 256, 256], P('slab', 'band')
- hartree: float32 [256, 256, 256], P('slab', 'band')
All inputs are finite; a program needn't handle non-finite values.
Results may differ from a plain program's by a relative error of at most 0.0019.
Values sent between devices are 32-bit elements; how exact they have to be, the bound alone decides.
No kernel may reach another device: no remote copies, remote signals or barrier semaphores. Data moves between devices by JAX's collectives and lax.ppermute only.
A program may use at most 128 MiB of HBM per device.

v0:
```python
import math

import jax
import jax.numpy as jnp
import numpy as np
from jax import lax
from jax.experimental import pallas as pl
from jax.experimental.pallas import tpu as pltpu
from jax.sharding import PartitionSpec as P


spacing = 0.08
axes = ("band", "slab")
planes = (9, 7)
cut = planes[1] // 2 + 1
piece_bytes = 576 << 10
spare_bytes = 4 << 20


def circle_tables(count):
    quarter = count // 4
    eighth = np.sin(2.0 * np.pi * np.arange(quarter + 1) / count)
    eighth[quarter] = 1.0
    first = np.concatenate([eighth[:quarter], eighth[:0:-1]])
    sine = np.concatenate([first, -first])
    cosine = np.roll(sine, -quarter)
    return cosine, sine


def split_table(table):
    high = table.astype(jnp.bfloat16)
    low = (table - high.astype(np.float64)).astype(jnp.bfloat16)
    return high, low


def dft_tables(count):
    cosine, sine = circle_tables(count)
    phases = np.arange(count)[:, None] * np.arange(count)[None, :] % count
    return cosine[phases], sine[phases]


def line_tables(count):
    cosine, sine = dft_tables(count)
    half = count // 2
    real_rows = cosine[:half].copy()
    imag_rows = -sine[:half]
    imag_rows[0] = cosine[half]
    return real_rows, imag_rows


def split(values):
    high = values.astype(jnp.bfloat16)
    low = (values - high.astype(jnp.float32)).astype(jnp.bfloat16)
    return high, low


def dot3(left, right, dims):
    first = jnp.concatenate([left[0], left[1], left[0]], axis=dims[0][0])
    second = jnp.concatenate([right[0], right[0], right[1]], axis=dims[1][0])
    return lax.dot_general(
        first, second, (dims, ((), ())), preferred_element_type=jnp.float32
    )


plain = ((1,), (0,))
rows_rows = ((1,), (1,))


def swap_blocks(parts):
    lane = lax.broadcasted_iota(jnp.int32, parts[0].shape, len(parts[0].shape) - 1)
    axis = len(parts[0].shape) - 1
    even = (lane // 32) % 2 == 0
    low = lane < 64
    pairs = []
    for first, second in ((parts[0], parts[1]), (parts[2], parts[3])):
        pairs.append(
            (
                jnp.where(even, first, pltpu.roll(second, 32, axis)),
                jnp.where(even, pltpu.roll(first, 96, axis), second),
            )
        )
    results = []
    for first, second in zip(*pairs):
        turned = pltpu.roll(jnp.where(low, second, first), 64, axis)
        results.append((jnp.where(low, first, turned), jnp.where(low, turned, second)))
    return [pair[0] for pair in results] + [pair[1] for pair in results]


def forward_kernel(
    own_ref, left_ref, right_ref, other_ref, line_ref, cross_ref, lines3_ref, lines1_ref, ahead_ref,
    high_ref, low_ref, density_ref, out_ref,
):
    depth = planes[0]
    density_ref[:depth] = (own_ref[...] + left_ref[...]) + (right_ref[...] + other_ref[...])
    lower = (line_ref[...] + cross_ref[1]) + lines3_ref[...]
    density_ref[depth : depth + cut] = lower[:cut] + lines1_ref[...]
    density_ref[depth + cut :] = lower[cut:] + ahead_ref[cut:]
    planes_of = [density_ref[z] for z in range(16)]
    rows = jnp.concatenate([planes_of[zh * 8 + zq] for zq in range(8) for zh in range(2)], axis=0)
    mean = jnp.sum(rows) * (1.0 / rows.size)
    lines = dot3((high_ref[...], low_ref[...]), split(rows - mean), rows_rows)
    zero = lax.broadcasted_iota(jnp.int32, (128, 512), 0) == 0
    real = lines[:128] + jnp.where(zero, mean * rows.shape[1], 0.0)
    imag = lines[128:]
    low = lax.broadcasted_iota(jnp.int32, (128, 128), 1) < 64
    for pair in range(4):
        a = real[:, pair * 128 : (pair + 1) * 128]
        b = imag[:, pair * 128 : (pair + 1) * 128]
        out_ref[pl.ds(2 * pair, 128, stride=8), :] = jnp.where(low, a, pltpu.roll(b, 64, 1))
        out_ref[pl.ds(2 * pair + 1, 128, stride=8), :] = jnp.where(low, pltpu.roll(a, 64, 1), b)


def plane_kernel(green_ref, message_ref, high_ref, low_ref, out_ref):
    count = 256
    stacked = (high_ref[...], low_ref[...])
    beside = [jnp.concatenate([table[:count], table[count:]], axis=1) for table in stacked]
    tile = jnp.sum(message_ref[...].reshape(128, 8, 128), axis=0)
    real_lane = lax.broadcasted_iota(jnp.int32, tile.shape, 1) < 64
    means = [
        jnp.sum(jnp.where(real_lane == keep, tile, 0.0)) * (1.0 / count**2) for keep in (True, False)
    ]
    reals, imags = [], []
    chunks = 1
    slabs = 16 // chunks
    rows = count // chunks
    for chunk in range(chunks):
        columns = [[], []]
        for group in range(2):
            parts = [
                message_ref[pl.ds((member * 16 + chunk * slabs) * 8, slabs * 8), :].reshape(
                    slabs, 8, 128
                )
                for member in range(group * 4, group * 4 + 4)
            ]
            blocks = swap_blocks(parts)
            for part in range(2):
                whole = jnp.stack([blocks[part * 2], blocks[part * 2 + 1]], axis=1)
                columns[part].append(whole.reshape(rows, 128))
        halves = [jnp.concatenate(columns[part], axis=1) - means[part] for part in range(2)]
        both = dot3(split(jnp.concatenate(halves, axis=0)), beside, plain)
        by_cos, by_sin = both[:, :count], both[:, count:]
        reals.append(by_cos[:rows] + by_sin[rows:])
        imags.append(by_cos[rows:] - by_sin[:rows])
    real = jnp.concatenate(reals, axis=0)
    imag = jnp.concatenate(imags, axis=0)
    both = dot3(stacked, split(jnp.concatenate([real, imag], axis=1)), plain)
    by_cos, by_sin = both[:count], both[count:]
    real = by_cos[:, :count] + by_sin[:, count:]
    imag = by_cos[:, count:] - by_sin[:, :count]
    zero = (lax.broadcasted_iota(jnp.int32, (count, count), 0) == 0) & (
        lax.broadcasted_iota(jnp.int32, (count, count), 1) == 0
    )
    real = real + jnp.where(zero, means[0] * count**2, 0.0)
    imag = imag + jnp.where(zero, means[1] * count**2, 0.0)
    green_a = green_ref[0]
    green_b = green_ref[1]
    operand = split(
        jnp.concatenate([real * green_a, imag * green_a, real * green_b, imag * green_b], axis=1)
    )
    both = dot3(stacked, operand, plain)
    by_cos, by_sin = both[:count], both[count:]
    real_a = by_cos[:, :count] - by_sin[:, count : 2 * count]
    imag_a = by_cos[:, count : 2 * count] + by_sin[:, :count]
    real_b = by_cos[:, 2 * count : 3 * count] - by_sin[:, 3 * count :]
    imag_b = by_cos[:, 3 * count :] + by_sin[:, 2 * count : 3 * count]
    for chunk in range(chunks):
        piece = slice(chunk * rows, (chunk + 1) * rows)
        pair = jnp.concatenate(
            [
                jnp.concatenate([real_a[piece], -imag_a[piece]], axis=1),
                jnp.concatenate([imag_b[piece], real_b[piece]], axis=1),
            ],
            axis=0,
        )
        result = dot3(split(pair), stacked, plain)
        for group in range(2):
            blocks = []
            for part in range(2):
                whole = result[part * rows : (part + 1) * rows, group * 128 : (group + 1) * 128]
                whole = whole.reshape(slabs, 2, 8, 128)
                blocks += [whole[:, 0], whole[:, 1]]
            for member, values in enumerate(swap_blocks(blocks), group * 4):
                place = pl.ds((member * 16 + chunk * slabs) * 8, slabs * 8)
                out_ref[place, :] = values.reshape(slabs * 8, 128)


def green_kernel(after_ref, out_ref):
    del after_ref
    count = 256
    rank = lax.axis_index("band") * lax.axis_size("slab") + lax.axis_index("slab")

    def signed(axis):
        index = lax.broadcasted_iota(jnp.int32, (count, count), axis)
        return jnp.where(index < count // 2, index, index - count).astype(jnp.float32)

    freq_z, freq_x = signed(0), signed(1)
    scale = (2.0 * math.pi / (count * spacing)) ** 2
    for place, freq in enumerate((rank, jnp.where(rank == 0, count // 2, rank))):
        freq_y = freq.astype(jnp.float32)
        wave_sq = scale * (freq_z * freq_z + freq_x * freq_x + freq_y * freq_y)
        anchor = wave_sq == 0.0
        out_ref[place] = jnp.where(
            anchor, 0.0, (4.0 * math.pi / count**3) / (wave_sq + anchor.astype(jnp.float32))
        )


def inverse_kernel(message_ref, high_ref, low_ref, out_ref):
    turned = [message_ref[pl.ds(zq, 128, stride=8), :].T for zq in range(8)]
    rows = jnp.concatenate(
        [jnp.concatenate([block[:64] for block in turned], axis=0),
         jnp.concatenate([block[64:] for block in turned], axis=0)], axis=1
    )
    lines = dot3(split(rows), (high_ref[...], low_ref[...]), plain)
    for zq in range(8):
        out_ref[zq] = lines[zq * 64 : zq * 64 + 32]
        out_ref[zq + 8] = lines[zq * 64 + 32 : zq * 64 + 64]


def density_kernel(pieces, occupation_ref, orbitals_ref, *refs):
    outs, (buffer, weights_ref, sems) = refs[:-3], refs[-3:]
    flat = [piece for group in pieces for piece in group]
    copies = []
    rank = lax.axis_index("band")
    for slot, (half, dx, dz) in enumerate(flat):
        block = (rank + 4 * dz) // 4 % 2 * 4 + (rank + dx) % 4
        depth = planes[half]
        source = orbitals_ref.at[:, pl.ds(half * planes[0], depth), pl.ds(block * 32, 32), :]
        target = buffer.at[slot, :, pl.ds(0, depth)]
        copies.append(pltpu.make_async_copy(source, target, sems.at[slot]))
    weigh = pltpu.make_async_copy(occupation_ref, weights_ref, sems.at[len(flat)])
    for copy in [weigh, *copies]:
        copy.start()
    weigh.wait()
    weights = [weights_ref[band] for band in range(4)]
    slot = 0
    for out, group in zip(outs, pieces):
        for place in range(len(group)):
            copies[slot].wait()
            total = None
            for band in range(4):
                values = buffer[slot, band, : planes[group[place][0]]].astype(jnp.float32)
                term = values * values * weights[band]
                total = term if total is None else total + term
            if len(group) == 1:
                out[...] = total
            else:
                out[place] = total
            slot += 1


def lines_kernel(cross_ref, line2_ref, line1_ref, ahead_out, behind_out):
    line = line2_ref[...] + cross_ref[0]
    ahead_out[:cut] = line[:cut]
    ahead_out[cut:] = line1_ref[cut:] + cross_ref[1, cut:]
    behind_out[...] = line[cut:]


def last_kernel(line_ref, cross_ref, behind_ref, out_ref):
    line = line_ref[...] + cross_ref[0]
    out_ref[:cut] = line[:cut]
    out_ref[cut:] = line[cut:] + behind_ref[...]


def partial_densities(orbitals, occupation, pieces):
    shapes = [
        pltpu.VMEM((len(g),) * (len(g) > 1) + (planes[g[0][0]], 32, 256), jnp.float32)
        for g in pieces
    ]
    count = sum(len(g) for g in pieces)
    limit = count * piece_bytes * 2 + spare_bytes
    return pl.pallas_call(
        lambda *refs: density_kernel(pieces, *refs),
        out_shape=shapes,
        in_specs=[pl.BlockSpec(memory_space=pltpu.HBM)] * 2,
        out_specs=[pl.BlockSpec(memory_space=pltpu.VMEM)] * len(shapes),
        scratch_shapes=[
            pltpu.VMEM((count, 4, max(planes), 32, 256), jnp.bfloat16),
            pltpu.SMEM((4,), jnp.float32),
            pltpu.SemaphoreType.DMA((count + 1,)),
        ],
        compiler_params=pltpu.CompilerParams(vmem_limit_bytes=limit),
    )(*[pltpu.with_memory_space_constraint(value, pltpu.HBM) for value in (occupation, orbitals)])


def vmem_call(kernel, out_shape, limit, operands):
    placed = [pltpu.with_memory_space_constraint(value, pltpu.VMEM) for value in operands]
    vmem = pl.BlockSpec(memory_space=pltpu.VMEM)
    return pl.pallas_call(
        kernel,
        out_shape=out_shape,
        in_specs=[vmem] * len(placed),
        out_specs=jax.tree.map(lambda shape: vmem, out_shape),
        compiler_params=pltpu.CompilerParams(vmem_limit_bytes=limit),
    )(*placed)


def exchange(message):
    return lax.all_to_all(message, axes, 0, 0, tiled=True)


def solve(orbitals, occupation):
    count = orbitals.shape[2]
    half = count // 2
    terms = band_sum(orbitals, occupation)

    forward_real, forward_imag = line_tables(count)
    tables = split_table(np.concatenate([forward_real, forward_imag]))
    block = jax.ShapeDtypeStruct((16, 32, count), jnp.float32)
    exchanged = pltpu.VMEM((half * 8, 128), jnp.float32)
    density = pltpu.VMEM((16, 32, count), jnp.float32)
    density, message = vmem_call(forward_kernel, [density, exchanged], 12 << 20, (*terms, *tables))
    green = pl.pallas_call(
        green_kernel,
        out_shape=pltpu.VMEM((2, count, count), jnp.float32),
        in_specs=[pl.BlockSpec(memory_space=pl.ANY)],
        out_specs=pl.BlockSpec(memory_space=pltpu.VMEM),
        compiler_params=pltpu.CompilerParams(vmem_limit_bytes=8 << 20),
        name="green",
    )(message)
    message = exchange(message)
    cosine, sine = dft_tables(count)
    tables = split_table(np.concatenate([cosine, sine]))
    message = vmem_call(plane_kernel, exchanged, 24 << 20, (green, message, *tables))
    message = exchange(message)

    weight = np.full((half, 1), 2.0)
    weight[0] = 1.0
    tables = split_table(np.concatenate([forward_real * weight, forward_imag * weight]))
    potential = vmem_call(inverse_kernel, block, 12 << 20, (message, *tables))
    return density, potential


def ring(dx, dz):
    pairs = []
    for z in range(2):
        for x in range(4):
            for slab in range(16):
                target = (z + dz) % 2 * 4 + (x + dx) % 4
                pairs.append(((z * 4 + x) * 16 + slab, target * 16 + slab))
    return pairs


def band_sum(orbitals, occupation):
    def send(values, dx, dz):
        return lax.ppermute(values, axes, ring(dx, dz))

    far0, far1, cross0 = partial_densities(
        orbitals, occupation, [[(0, 2, 0)], [(0, 2, 1)], [(1, 2, 1), (1, 1, 1)]]
    )
    far0 = send(far0, 1, 0)
    far1 = send(far1, -1, 0)
    cross0 = send(cross0, 0, 1)
    right1, left0, cross1 = partial_densities(
        orbitals, occupation, [[(0, 1, 1)], [(0, 3, 0)], [(1, 3, 1), (1, 0, 1)]]
    )
    right1 = send(right1, 1, 0)
    left0 = send(left0, -1, 0)
    left1, right0, line2, line1, line3, own1, own0, line0 = partial_densities(
        orbitals,
        occupation,
        [
            [(0, 3, 1)],
            [(0, 1, 0)],
            [(1, 2, 0)],
            [(1, 1, 0)],
            [(1, 3, 0)],
            [(0, 0, 1)],
            [(0, 0, 0)],
            [(1, 0, 0)],
        ],
    )
    left1 = send(left1 + far1, -1, 0)
    right0 = send(right0 + far0, 1, 0)
    cross1 = send(cross1, 0, 1)
    ahead, behind = vmem_call(
        lines_kernel,
        [pltpu.VMEM((depth, 32, 256), jnp.float32) for depth in (planes[1], planes[1] - cut)],
        8 << 20,
        (cross0, line2, line1),
    )
    ahead = send(ahead, 1, 0)
    behind = send(behind, -1, 0)
    other = send(own1 + right1 + left1, 0, 1)
    lines1 = send(line1[:cut] + cross0[1, :cut] + ahead[:cut], 1, 0)
    to_left = vmem_call(
        last_kernel, pltpu.VMEM((planes[1], 32, 256), jnp.float32), 8 << 20, (line3, cross1, behind)
    )
    lines3 = send(to_left, -1, 0)
    return (own0, left0, right0, other, line0, cross1, lines3, lines1, ahead)


def solution(mesh):
    in_specs = (P("band", "slab", None, None), P("band"))
    out_specs = (P("slab", "band", None), P("slab", "band", None))
    return jax.shard_map(solve, mesh=mesh, in_specs=in_specs, out_specs=out_specs, check_vma=False)
```

profile of v0, /device:TPU:1, one launch (start us, length us, event | category | flops | bytes accessed | tf_op | source)
XLA Modules:
  0.0 97.2 jit_solution(17284067101827280178)
XLA Ops:
  0.6 1.7 %shard_map.97 = (f32[9,32,256]{2,1,0:T(8,128)S(1)}, f32[9,32,256]{2,1,0:T(8,128)S(1)}, f32[2,7,32,256]{3,2,1,0:T(8,128)S(1)}) custom-call(f32[4]{0:T(128)} %refs_0_.5, bf16[4,16,256,256]{3,2,1,0:T(8,128)(2,1)} %refs_1_.5), custom_call_target="tpu_custom_call" | custom-call | tf_op jit(solution)/shard_map/pallas_call | solution.py:271
  2.3 3.4 %collective-permute-start.4 = (f32[9,32,256]{2,1,0:T(8,128)S(1)}, f32[9,32,256]{2,1,0:T(8,128)S(1)}, u32[]{:S(2)}, u32[]{:S(2)}) collective-permute-start(f32[9,32,256]{2,1,0:T(8,128)S(1)} %get-tuple-element.27), channel_id=1, source_target_pairs={{0,48},{1,49},{2,50},{3,51},{4,52},{5,53},{6,54},{7,55},{8,56},{9,... | collective-permute-start | bytes 884744 | tf_op jit(solution)/shard_map/ppermute | solution.py:345
  5.7 3.6 %collective-permute-start.8 = (f32[2,7,32,256]{3,2,1,0:T(8,128)S(1)}, f32[2,7,32,256]{3,2,1,0:T(8,128)S(1)}, u32[]{:S(2)}, u32[]{:S(2)}) collective-permute-start(f32[2,7,32,256]{3,2,1,0:T(8,128)S(1)} %get-tuple-element.31), channel_id=1, source_target_pairs={{0,64},{1,65},{2,66},{3,67},{4,68},{5,69},{6,70},{7,71},{8,72},{9,... | collective-permute-start | bytes 1376264 | tf_op jit(solution)/shard_map/ppermute | solution.py:345
  9.3 1.7 %shard_map.96 = (f32[9,32,256]{2,1,0:T(8,128)S(1)}, f32[9,32,256]{2,1,0:T(8,128)S(1)}, f32[2,7,32,256]{3,2,1,0:T(8,128)S(1)}) custom-call(f32[4]{0:T(128)} %refs_0_.5, bf16[4,16,256,256]{3,2,1,0:T(8,128)(2,1)} %refs_1_.5), custom_call_target="tpu_custom_call" | custom-call | tf_op jit(solution)/shard_map/pallas_call | solution.py:271
  11.0 0.0 copy-start.4
  11.0 0.0 copy-start.5
  11.0 0.1 collective-permute-start.7
  11.1 0.1 collective-permute-start.1
  11.2 0.0 copy-start
  11.2 0.2 collective-permute-start.3
  11.4 2.4 %shard_map.95 = (f32[9,32,256]{2,1,0:T(8,128)S(1)}, f32[9,32,256]{2,1,0:T(8,128)S(1)}, f32[7,32,256]{2,1,0:T(8,128)S(1)}, f32[7,32,256]{2,1,0:T(8,128)S(1)}, f32...) custom-call(f32[4]{0:T(128)} %refs_0_.5, ...), custom_call_target="tpu_custom_call" | custom-call | tf_op jit(solution)/shard_map/pallas_call | solution.py:271
  13.9 2.7 %collective-permute-start.5 = (f32[9,32,256]{2,1,0:T(8,128)S(1)}, f32[9,32,256]{2,1,0:T(8,128)S(1)}, u32[]{:S(2)}, u32[]{:S(2)}) collective-permute-start(f32[9,32,256]{2,1,0:T(8,128)S(1)} %add.20), channel_id=1, source_target_pairs={{0,48},{1,49},{2,50},{3,51},{4,52},{5,53},{6,54},{7,55},{8,56},{9,... | collective-permute-start | bytes 884744 | tf_op jit(solution)/shard_map/ppermute | solution.py:345
  16.6 2.7 %collective-permute-done.8.cross_ref = f32[2,7,32,256]{3,2,1,0:T(8,128)S(1)} collective-permute-done((f32[2,7,32,256]{3,2,1,0:T(8,128)S(1)}, f32[2,7,32,256]{3,2,1,0:T(8,128)S(1)}, u32[]{:S(2)}, u32[]{:S(2)}) %collective-permute-start.8) | collective-permute-done | bytes 458784 | tf_op jit(solution)/shard_map/ppermute | solution.py:345
  19.3 0.6 collective-permute-start.9
  19.9 0.3 collective-permute-start
  20.2 8.9 %collective-permute-done.7.cross_ref = f32[2,7,32,256]{3,2,1,0:T(8,128)S(1)} collective-permute-done((f32[2,7,32,256]{3,2,1,0:T(8,128)S(1)}, f32[2,7,32,256]{3,2,1,0:T(8,128)S(1)}, u32[]{:S(2)}, u32[]{:S(2)}) %collective-permute-start.7) | collective-permute-done | bytes 458784 | tf_op jit(solution)/shard_map/ppermute | solution.py:345
  29.1 0.2 collective-permute-start.11
  29.3 2.6 %collective-permute-start.10 = (f32[7,32,256]{2,1,0:T(8,128)S(1)}, f32[7,32,256]{2,1,0:T(8,128)S(1)}, u32[]{:S(2)}, u32[]{:S(2)}) collective-permute-start(f32[7,32,256]{2,1,0:T(8,128)S(1)} %shard_map.99), channel_id=1, source_target_pairs={{0,48},{1,49},{2,50},{3,51},{4,52},{5,53},{6,54},{7,55},{8,56},{9,... | collective-permute-start | bytes 688136 | tf_op jit(solution)/shard_map/ppermute | solution.py:345
  31.9 0.1 add_add_fusion
  32.0 2.8 %collective-permute-start.6 = (f32[9,32,256]{2,1,0:T(8,128)S(1)}, f32[9,32,256]{2,1,0:T(8,128)S(1)}, u32[]{:S(2)}, u32[]{:S(2)}) collective-permute-start(f32[9,32,256]{2,1,0:T(8,128)S(1)} %add_add_fusion), channel_id=1, source_target_pairs={{0,64},{1,65},{2,66},{3,67},{4,68},{5,69},{6,70},{7,71},{8,72},{9,... | collective-permute-start | bytes 884744 | tf_op jit(solution)/shard_map/ppermute | solution.py:345
  34.7 7.5 %collective-permute-done.11.ahead_ref = f32[7,32,256]{2,1,0:T(8,128)S(1)} collective-permute-done((f32[7,32,256]{2,1,0:T(8,128)S(1)}, f32[7,32,256]{2,1,0:T(8,128)S(1)}, u32[]{:S(2)}, u32[]{:S(2)}) %collective-permute-start.11) | collective-permute-done | bytes 229408 | tf_op jit(solution)/shard_map/ppermute | solution.py:345
  42.3 0.1 collective-permute-start.12
  42.4 5.0 %collective-permute-done.12.lines1_ref = f32[4,32,256]{2,1,0:T(8,128)S(1)} collective-permute-done((f32[4,32,256]{2,1,0:T(8,128)S(1)}, f32[4,32,256]{2,1,0:T(8,128)S(1)}, u32[]{:S(2)}, u32[]{:S(2)}) %collective-permute-start.12) | collective-permute-done | bytes 131104 | tf_op jit(solution)/shard_map/ppermute | solution.py:345
  47.4 1.7 %shard_map.100 = (f32[16,32,256]{2,1,0:T(8,128)S(1)}, f32[1024,128]{1,0:T(8,128)}) custom-call(f32[9,32,256]{2,1,0:T(8,128)S(1)} %get-tuple-element.20.own_ref, f32[9,32,256]{2,1,0:T(8,128)S(1)} %collective-permute-done.left_ref, f32[9,32,256]{2,1,0:T(8,128)S(1)} %collective-permute-done.2.right_ref, f32[9,32,256]{2,1,0:T(8,128)S(1)} %collective-permute-done.6.other_ref, ...), custom_call_target="tpu_custom_call" | custom-call | tf_op jit(solution)/shard_map/pallas_call | solution.py:288
  49.1 10.2 %all-to-all-start = ((f32[128,8,128]{2,1,0:T(8,128)}), f32[128,8,128]{2,1,0:T(8,128)S(1)}, u32[]{:S(2)}, u32[]{:S(2)}) async-start(f32[128,8,128]{2,1,0:T(8,128)} %bitcast.1), calls=%async_computation | async-start | bytes 1048576 | tf_op jit(solution)/shard_map/all_to_all | solution.py:298
  59.3 0.2 green.1.green_ref
  59.5 13.9 %all-to-all-done = f32[128,8,128]{2,1,0:T(8,128)S(1)} async-done(((f32[128,8,128]{2,1,0:T(8,128)}), f32[128,8,128]{2,1,0:T(8,128)S(1)}, u32[]{:S(2)}, u32[]{:S(2)}) %all-to-all-start) | async-done | bytes 524320 | tf_op jit(solution)/shard_map/all_to_all | solution.py:298
  73.4 4.5 %shard_map.101 = f32[1024,128]{1,0:T(8,128)} custom-call(f32[2,256,256]{2,1,0:T(8,128)S(1)} %green.1.green_ref, f32[1024,128]{1,0:T(8,128)S(1)} %bitcast.11, bf16[512,256]{1,0:T(8,128)(2,1)S(1)} %copy-done, bf16[512,256]{1,0:T(8,128)(2,1)S(1)} %copy-done.1), custom_call_target="tpu_custom_call" | custom-call | tf_op jit(solution)/shard_map/pallas_call | solution.py:288
  77.9 3.9 %all-to-all-start.1 = ((f32[128,8,128]{2,1,0:T(8,128)}), f32[128,8,128]{2,1,0:T(8,128)S(1)}, u32[]{:S(2)}, u32[]{:S(2)}) async-start(f32[128,8,128]{2,1,0:T(8,128)} %bitcast.3), calls=%async_computation.1 | async-start | bytes 1048576 | tf_op jit(solution)/shard_map/all_to_all | solution.py:298
  81.8 0.8 copy.10
  82.6 13.3 %all-to-all-done.1 = f32[128,8,128]{2,1,0:T(8,128)S(1)} async-done(((f32[128,8,128]{2,1,0:T(8,128)}), f32[128,8,128]{2,1,0:T(8,128)S(1)}, u32[]{:S(2)}, u32[]{:S(2)}) %all-to-all-start.1) | async-done | bytes 524320 | tf_op jit(solution)/shard_map/all_to_all | solution.py:298
  95.9 1.2 %shard_map.102 = f32[16,32,256]{2,1,0:T(8,128)} custom-call(f32[1024,128]{1,0:T(8,128)S(1)} %bitcast.10, bf16[256,256]{1,0:T(8,128)(2,1)S(1)} %copy-done.2, bf16[256,256]{1,0:T(8,128)(2,1)S(1)} %copy-done.3), custom_call_target="tpu_custom_call" | custom-call | tf_op jit(solution)/shard_map/pallas_call | solution.py:288
  (24 shorter events, 0.2 us)
Async XLA Ops:
  2.3 11.4 %collective-permute-start.4 = (f32[9,32,256]{2,1,0:T(8,128)S(1)}, f32[9,32,256]{2,1,0:T(8,128)S(1)}, u32[]{:S(2)}, u32[]{:S(2)}) collective-permute-start(f32[9,32,256]{2,1,0:T(8,128)S(1)} %get-tuple-element.27), channel_id=1, source_target_pairs={{0,48},{1,49},{2,50},{3,51},{4,52},{5,53},{6,54},{7,55},{8,56},{9,... | collective-permute-start | bytes 884744 | tf_op jit(solution)/shard_map/ppermute | solution.py:345
  5.7 13.5 %collective-permute-start.8 = (f32[2,7,32,256]{3,2,1,0:T(8,128)S(1)}, f32[2,7,32,256]{3,2,1,0:T(8,128)S(1)}, u32[]{:S(2)}, u32[]{:S(2)}) collective-permute-start(f32[2,7,32,256]{3,2,1,0:T(8,128)S(1)} %get-tuple-element.31), channel_id=1, source_target_pairs={{0,64},{1,65},{2,66},{3,67},{4,68},{5,69},{6,70},{7,71},{8,72},{9,... | collective-permute-start | bytes 1376264 | tf_op jit(solution)/shard_map/ppermute | solution.py:345
  11.0 36.4 %copy-start.4 = (bf16[256,256]{1,0:T(8,128)(2,1)S(1)}, bf16[256,256]{1,0:T(8,128)(2,1)}, u32[]{:S(2)}) copy-start(bf16[256,256]{1,0:T(8,128)(2,1)} %constant.12.clone.high_ref) | copy-start | bytes 393220
  11.0 36.4 %copy-start.5 = (bf16[256,256]{1,0:T(8,128)(2,1)S(1)}, bf16[256,256]{1,0:T(8,128)(2,1)}, u32[]{:S(2)}) copy-start(bf16[256,256]{1,0:T(8,128)(2,1)} %constant.13.clone.low_ref) | copy-start | bytes 393220
  11.0 18.1 %collective-permute-start.7 = (f32[2,7,32,256]{3,2,1,0:T(8,128)S(1)}, f32[2,7,32,256]{3,2,1,0:T(8,128)S(1)}, u32[]{:S(2)}, u32[]{:S(2)}) collective-permute-start(f32[2,7,32,256]{3,2,1,0:T(8,128)S(1)} %get-tuple-element.29), channel_id=1, source_target_pairs={{0,64},{1,65},{2,66},{3,67},{4,68},{5,69},{6,70},{7,71},{8,72},{9,... | collective-permute-start | bytes 1376264 | tf_op jit(solution)/shard_map/ppermute | solution.py:345
  11.1 8.8 %collective-permute-start.1 = (f32[9,32,256]{2,1,0:T(8,128)S(1)}, f32[9,32,256]{2,1,0:T(8,128)S(1)}, u32[]{:S(2)}, u32[]{:S(2)}) collective-permute-start(f32[9,32,256]{2,1,0:T(8,128)S(1)} %get-tuple-element.23), channel_id=1, source_target_pairs={{0,16},{1,17},{2,18},{3,19},{4,20},{5,21},{6,22},{7,23},{8,24},{9,... | collective-permute-start | bytes 884744 | tf_op jit(solution)/shard_map/ppermute | solution.py:345
  11.2 62.2 %copy-start = (bf16[512,256]{1,0:T(8,128)(2,1)S(1)}, bf16[512,256]{1,0:T(8,128)(2,1)}, u32[]{:S(2)}) copy-start(bf16[512,256]{1,0:T(8,128)(2,1)} %constant.14.clone.high_ref) | copy-start | bytes 786436
  11.2 62.1 %copy-start.1 = (bf16[512,256]{1,0:T(8,128)(2,1)S(1)}, bf16[512,256]{1,0:T(8,128)(2,1)}, u32[]{:S(2)}) copy-start(bf16[512,256]{1,0:T(8,128)(2,1)} %constant.15.clone.low_ref) | copy-start | bytes 786436
  11.2 18.1 %collective-permute-start.3 = (f32[9,32,256]{2,1,0:T(8,128)S(1)}, f32[9,32,256]{2,1,0:T(8,128)S(1)}, u32[]{:S(2)}, u32[]{:S(2)}) collective-permute-start(f32[9,32,256]{2,1,0:T(8,128)S(1)} %get-tuple-element.25), channel_id=1, source_target_pairs={{0,16},{1,17},{2,18},{3,19},{4,20},{5,21},{6,22},{7,23},{8,24},{9,... | collective-permute-start | bytes 884744 | tf_op jit(solution)/shard_map/ppermute | solution.py:345
  13.8 82.2 %copy-start.2 = (bf16[256,256]{1,0:T(8,128)(2,1)S(1)}, bf16[256,256]{1,0:T(8,128)(2,1)}, u32[]{:S(2)}) copy-start(bf16[256,256]{1,0:T(8,128)(2,1)} %constant.16.clone.high_ref) | copy-start | bytes 393220
  13.8 82.2 %copy-start.3 = (bf16[256,256]{1,0:T(8,128)(2,1)S(1)}, bf16[256,256]{1,0:T(8,128)(2,1)}, u32[]{:S(2)}) copy-start(bf16[256,256]{1,0:T(8,128)(2,1)} %constant.17.clone.low_ref) | copy-start | bytes 393220
  13.9 18.0 %collective-permute-start.5 = (f32[9,32,256]{2,1,0:T(8,128)S(1)}, f32[9,32,256]{2,1,0:T(8,128)S(1)}, u32[]{:S(2)}, u32[]{:S(2)}) collective-permute-start(f32[9,32,256]{2,1,0:T(8,128)S(1)} %add.20), channel_id=1, source_target_pairs={{0,48},{1,49},{2,50},{3,51},{4,52},{5,53},{6,54},{7,55},{8,56},{9,... | collective-permute-start | bytes 884744 | tf_op jit(solution)/shard_map/ppermute | solution.py:345
  19.3 9.8 %collective-permute-start.9 = (f32[3,32,256]{2,1,0:T(8,128)S(1)}, f32[3,32,256]{2,1,0:T(8,128)S(1)}, u32[]{:S(2)}, u32[]{:S(2)}) collective-permute-start(f32[3,32,256]{2,1,0:T(8,128)S(1)} %get-tuple-element.34), channel_id=1, source_target_pairs={{0,48},{1,49},{2,50},{3,51},{4,52},{5,53},{6,54},{7,55},{8,56},{9,... | collective-permute-start | bytes 294920 | tf_op jit(solution)/shard_map/ppermute | solution.py:345
  19.9 22.4 %collective-permute-start = (f32[9,32,256]{2,1,0:T(8,128)S(1)}, f32[9,32,256]{2,1,0:T(8,128)S(1)}, u32[]{:S(2)}, u32[]{:S(2)}) collective-permute-start(f32[9,32,256]{2,1,0:T(8,128)S(1)} %get-tuple-element.21), channel_id=1, source_target_pairs={{0,48},{1,49},{2,50},{3,51},{4,52},{5,53},{6,54},{7,55},{8,56},{9,... | collective-permute-start | bytes 884744 | tf_op jit(solution)/shard_map/ppermute | solution.py:345
  29.1 13.3 %collective-permute-start.2 = (f32[9,32,256]{2,1,0:T(8,128)S(1)}, f32[9,32,256]{2,1,0:T(8,128)S(1)}, u32[]{:S(2)}, u32[]{:S(2)}) collective-permute-start(f32[9,32,256]{2,1,0:T(8,128)S(1)} %add.18), channel_id=1, source_target_pairs={{0,16},{1,17},{2,18},{3,19},{4,20},{5,21},{6,22},{7,23},{8,24},{9,... | collective-permute-start | bytes 884744 | tf_op jit(solution)/shard_map/ppermute | solution.py:345
  29.1 13.2 %collective-permute-start.11 = (f32[7,32,256]{2,1,0:T(8,128)S(1)}, f32[7,32,256]{2,1,0:T(8,128)S(1)}, u32[]{:S(2)}, u32[]{:S(2)}) collective-permute-start(f32[7,32,256]{2,1,0:T(8,128)S(1)} %get-tuple-element.35), channel_id=1, source_target_pairs={{0,16},{1,17},{2,18},{3,19},{4,20},{5,21},{6,22},{7,23},{8,24},{9,... | collective-permute-start | bytes 688136 | tf_op jit(solution)/shard_map/ppermute | solution.py:345
  29.3 13.1 %collective-permute-start.10 = (f32[7,32,256]{2,1,0:T(8,128)S(1)}, f32[7,32,256]{2,1,0:T(8,128)S(1)}, u32[]{:S(2)}, u32[]{:S(2)}) collective-permute-start(f32[7,32,256]{2,1,0:T(8,128)S(1)} %shard_map.99), channel_id=1, source_target_pairs={{0,48},{1,49},{2,50},{3,51},{4,52},{5,53},{6,54},{7,55},{8,56},{9,... | collective-permute-start | bytes 688136 | tf_op jit(solution)/shard_map/ppermute | solution.py:345
  32.0 15.4 %collective-permute-start.6 = (f32[9,32,256]{2,1,0:T(8,128)S(1)}, f32[9,32,256]{2,1,0:T(8,128)S(1)}, u32[]{:S(2)}, u32[]{:S(2)}) collective-permute-start(f32[9,32,256]{2,1,0:T(8,128)S(1)} %add_add_fusion), channel_id=1, source_target_pairs={{0,64},{1,65},{2,66},{3,67},{4,68},{5,69},{6,70},{7,71},{8,72},{9,... | collective-permute-start | bytes 884744 | tf_op jit(solution)/shard_map/ppermute | solution.py:345
  42.3 5.1 %collective-permute-start.12 = (f32[4,32,256]{2,1,0:T(8,128)S(1)}, f32[4,32,256]{2,1,0:T(8,128)S(1)}, u32[]{:S(2)}, u32[]{:S(2)}) collective-permute-start(f32[4,32,256]{2,1,0:T(8,128)S(1)} %slice_add_fusion), channel_id=1, source_target_pairs={{0,16},{1,17},{2,18},{3,19},{4,20},{5,21},{6,22},{7,23},{8,24},{9,... | collective-permute-start | bytes 393224 | tf_op jit(solution)/shard_map/ppermute | solution.py:345
  49.1 24.2 %all-to-all-start = ((f32[128,8,128]{2,1,0:T(8,128)}), f32[128,8,128]{2,1,0:T(8,128)S(1)}, u32[]{:S(2)}, u32[]{:S(2)}) async-start(f32[128,8,128]{2,1,0:T(8,128)} %bitcast.1), calls=%async_computation | async-start | bytes 1048576 | tf_op jit(solution)/shard_map/all_to_all | solution.py:298
  77.9 18.0 %all-to-all-start.1 = ((f32[128,8,128]{2,1,0:T(8,128)}), f32[128,8,128]{2,1,0:T(8,128)S(1)}, u32[]{:S(2)}, u32[]{:S(2)}) async-start(f32[128,8,128]{2,1,0:T(8,128)} %bitcast.3), calls=%async_computation.1 | async-start | bytes 1048576 | tf_op jit(solution)/shard_map/all_to_all | solution.py:298
where the time goes:
time: 97.5 us; the launch traced here: 97.2 us
  waiting for transfers between devices  51.3 us (53%)
  starting transfers between devices  30.5 us (31%)
  Pallas kernels  13.5 us (14%)
    all_to_all x2, waiting for transfers between devices, exchange(): return lax.all_to_all(message, axes, 0, 0, tiled=True)  27.2 us
    ppermute x13, waiting for transfers between devices, send(): return lax.ppermute(values, axes, ring(dx, dz))  24.1 us
    ppermute x13, starting transfers between devices, send(): return lax.ppermute(values, axes, ring(dx, dz))  16.5 us
    all_to_all x2, starting transfers between devices, exchange(): return lax.all_to_all(message, axes, 0, 0, tiled=True)  14.1 us
    pallas_call x5, Pallas kernels, vmem_call(): pl.pallas_call(kernel, out_shape=out_shape, in_specs=[vmem] * len(placed)...  7.56 us
    pallas_call x3, Pallas kernels, partial_densities(): pl.pallas_call(lambda *refs: density_kernel(pieces, *refs), out_shape=sha...  5.76 us
  transfers between devices with their start and end apart: 15, of which 6 were waited for; matrix products, arithmetic and copies ran while one was open for 1% of the time, Pallas kernels for 4%

commit v1 on v0

--- a/solution.py
+++ b/solution.py
@@ -97,7 +97,8 @@
     density_ref[depth + cut :] = lower[cut:] + ahead_ref[cut:]
     planes_of = [density_ref[z] for z in range(16)]
     rows = jnp.concatenate([planes_of[zh * 8 + zq] for zq in range(8) for zh in range(2)], axis=0)
-    mean = jnp.sum(rows) * (1.0 / rows.size)
+    some = rows[:128]
+    mean = jnp.sum(some) * (1.0 / some.size)
     lines = dot3((high_ref[...], low_ref[...]), split(rows - mean), rows_rows)
     zero = lax.broadcasted_iota(jnp.int32, (128, 512), 0) == 0
     real = lines[:128] + jnp.where(zero, mean * rows.shape[1], 0.0)
@@ -106,8 +107,9 @@
     for pair in range(4):
         a = real[:, pair * 128 : (pair + 1) * 128]
         b = imag[:, pair * 128 : (pair + 1) * 128]
-        out_ref[pl.ds(2 * pair, 128, stride=8), :] = jnp.where(low, a, pltpu.roll(b, 64, 1))
-        out_ref[pl.ds(2 * pair + 1, 128, stride=8), :] = jnp.where(low, pltpu.roll(a, 64, 1), b)
+        turned = pltpu.roll(jnp.where(low, b, a), 64, 1)
+        out_ref[pl.ds(2 * pair, 128, stride=8), :] = jnp.where(low, a, turned)
+        out_ref[pl.ds(2 * pair + 1, 128, stride=8), :] = jnp.where(low, turned, b)
 
 
 def plane_kernel(green_ref, message_ref, high_ref, low_ref, out_ref):

time: 97.5 us -> 97.2 us (level)
  no operation moved by 1% of the time
where the time goes in v1:
time: 97.2 us; the launch traced here: 96.9 us
  waiting for transfers between devices  51.3 us (53%)
  starting transfers between devices  30.5 us (31%)
  Pallas kernels  13.3 us (14%)
    all_to_all x2, waiting for transfers between devices, exchange(): return lax.all_to_all(message, axes, 0, 0, tiled=True)  27.2 us
    ppermute x13, waiting for transfers between devices, send(): return lax.ppermute(values, axes, ring(dx, dz))  24.1 us
    ppermute x13, starting transfers between devices, send(): return lax.ppermute(values, axes, ring(dx, dz))  16.5 us
    all_to_all x2, starting transfers between devices, exchange(): return lax.all_to_all(message, axes, 0, 0, tiled=True)  14.1 us
    pallas_call x5, Pallas kernels, vmem_call(): pl.pallas_call(kernel, out_shape=out_shape, in_specs=[vmem] * len(placed)...  7.33 us
    pallas_call x3, Pallas kernels, partial_densities(): pl.pallas_call(lambda *refs: density_kernel(pieces, *refs), out_shape=sha...  5.76 us
  transfers between devices with their start and end apart: 15, of which 6 were waited for; matrix products, arithmetic and copies ran while one was open for 1% of the time, Pallas kernels for 4%

profile of v1, /device:TPU:1, one launch (start us, length us, event | category | flops | bytes accessed | tf_op | source)
XLA Modules:
  0.0 96.9 jit_solution(5615799317584554674)
XLA Ops:
  0.6 1.7 %shard_map.97 = (f32[9,32,256]{2,1,0:T(8,128)S(1)}, f32[9,32,256]{2,1,0:T(8,128)S(1)}, f32[2,7,32,256]{3,2,1,0:T(8,128)S(1)}) custom-call(f32[4]{0:T(128)} %refs_0_.5, bf16[4,16,256,256]{3,2,1,0:T(8,128)(2,1)} %refs_1_.5), custom_call_target="tpu_custom_call" | custom-call | tf_op jit(solution)/shard_map/pallas_call | solution.py:273
  2.3 3.4 %collective-permute-start.4 = (f32[9,32,256]{2,1,0:T(8,128)S(1)}, f32[9,32,256]{2,1,0:T(8,128)S(1)}, u32[]{:S(2)}, u32[]{:S(2)}) collective-permute-start(f32[9,32,256]{2,1,0:T(8,128)S(1)} %get-tuple-element.27), channel_id=1, source_target_pairs={{0,48},{1,49},{2,50},{3,51},{4,52},{5,53},{6,54},{7,55},{8,56},{9,... | collective-permute-start | bytes 884744 | tf_op jit(solution)/shard_map/ppermute | solution.py:347
  5.7 3.6 %collective-permute-start.8 = (f32[2,7,32,256]{3,2,1,0:T(8,128)S(1)}, f32[2,7,32,256]{3,2,1,0:T(8,128)S(1)}, u32[]{:S(2)}, u32[]{:S(2)}) collective-permute-start(f32[2,7,32,256]{3,2,1,0:T(8,128)S(1)} %get-tuple-element.31), channel_id=1, source_target_pairs={{0,64},{1,65},{2,66},{3,67},{4,68},{5,69},{6,70},{7,71},{8,72},{9,... | collective-permute-start | bytes 1376264 | tf_op jit(solution)/shard_map/ppermute | solution.py:347
  9.3 1.7 %shard_map.96 = (f32[9,32,256]{2,1,0:T(8,128)S(1)}, f32[9,32,256]{2,1,0:T(8,128)S(1)}, f32[2,7,32,256]{3,2,1,0:T(8,128)S(1)}) custom-call(f32[4]{0:T(128)} %refs_0_.5, bf16[4,16,256,256]{3,2,1,0:T(8,128)(2,1)} %refs_1_.5), custom_call_target="tpu_custom_call" | custom-call | tf_op jit(solution)/shard_map/pallas_call | solution.py:273
  11.0 0.0 copy-start.4
  11.0 0.0 copy-start.5
  11.0 0.1 collective-permute-start.7
  11.1 0.1 collective-permute-start.1
  11.2 0.0 copy-start
  11.2 0.2 collective-permute-start.3
  11.4 2.4 %shard_map.95 = (f32[9,32,256]{2,1,0:T(8,128)S(1)}, f32[9,32,256]{2,1,0:T(8,128)S(1)}, f32[7,32,256]{2,1,0:T(8,128)S(1)}, f32[7,32,256]{2,1,0:T(8,128)S(1)}, f32...) custom-call(f32[4]{0:T(128)} %refs_0_.5, ...), custom_call_target="tpu_custom_call" | custom-call | tf_op jit(solution)/shard_map/pallas_call | solution.py:273
  13.9 2.7 %collective-permute-start.5 = (f32[9,32,256]{2,1,0:T(8,128)S(1)}, f32[9,32,256]{2,1,0:T(8,128)S(1)}, u32[]{:S(2)}, u32[]{:S(2)}) collective-permute-start(f32[9,32,256]{2,1,0:T(8,128)S(1)} %add.20), channel_id=1, source_target_pairs={{0,48},{1,49},{2,50},{3,51},{4,52},{5,53},{6,54},{7,55},{8,56},{9,... | collective-permute-start | bytes 884744 | tf_op jit(solution)/shard_map/ppermute | solution.py:347
  16.6 2.7 %collective-permute-done.8.cross_ref = f32[2,7,32,256]{3,2,1,0:T(8,128)S(1)} collective-permute-done((f32[2,7,32,256]{3,2,1,0:T(8,128)S(1)}, f32[2,7,32,256]{3,2,1,0:T(8,128)S(1)}, u32[]{:S(2)}, u32[]{:S(2)}) %collective-permute-start.8) | collective-permute-done | bytes 458784 | tf_op jit(solution)/shard_map/ppermute | solution.py:347
  19.3 0.6 collective-permute-start.9
  19.9 0.3 collective-permute-start
  20.2 8.9 %collective-permute-done.7.cross_ref = f32[2,7,32,256]{3,2,1,0:T(8,128)S(1)} collective-permute-done((f32[2,7,32,256]{3,2,1,0:T(8,128)S(1)}, f32[2,7,32,256]{3,2,1,0:T(8,128)S(1)}, u32[]{:S(2)}, u32[]{:S(2)}) %collective-permute-start.7) | collective-permute-done | bytes 458784 | tf_op jit(solution)/shard_map/ppermute | solution.py:347
  29.1 0.2 collective-permute-start.11
  29.3 2.6 %collective-permute-start.10 = (f32[7,32,256]{2,1,0:T(8,128)S(1)}, f32[7,32,256]{2,1,0:T(8,128)S(1)}, u32[]{:S(2)}, u32[]{:S(2)}) collective-permute-start(f32[7,32,256]{2,1,0:T(8,128)S(1)} %shard_map.99), channel_id=1, source_target_pairs={{0,48},{1,49},{2,50},{3,51},{4,52},{5,53},{6,54},{7,55},{8,56},{9,... | collective-permute-start | bytes 688136 | tf_op jit(solution)/shard_map/ppermute | solution.py:347
  31.9 0.1 add_add_fusion
  32.0 2.8 %collective-permute-start.6 = (f32[9,32,256]{2,1,0:T(8,128)S(1)}, f32[9,32,256]{2,1,0:T(8,128)S(1)}, u32[]{:S(2)}, u32[]{:S(2)}) collective-permute-start(f32[9,32,256]{2,1,0:T(8,128)S(1)} %add_add_fusion), channel_id=1, source_target_pairs={{0,64},{1,65},{2,66},{3,67},{4,68},{5,69},{6,70},{7,71},{8,72},{9,... | collective-permute-start | bytes 884744 | tf_op jit(solution)/shard_map/ppermute | solution.py:347
  34.7 7.5 %collective-permute-done.11.ahead_ref = f32[7,32,256]{2,1,0:T(8,128)S(1)} collective-permute-done((f32[7,32,256]{2,1,0:T(8,128)S(1)}, f32[7,32,256]{2,1,0:T(8,128)S(1)}, u32[]{:S(2)}, u32[]{:S(2)}) %collective-permute-start.11) | collective-permute-done | bytes 229408 | tf_op jit(solution)/shard_map/ppermute | solution.py:347
  42.3 0.1 collective-permute-start.12
  42.4 5.0 %collective-permute-done.12.lines1_ref = f32[4,32,256]{2,1,0:T(8,128)S(1)} collective-permute-done((f32[4,32,256]{2,1,0:T(8,128)S(1)}, f32[4,32,256]{2,1,0:T(8,128)S(1)}, u32[]{:S(2)}, u32[]{:S(2)}) %collective-permute-start.12) | collective-permute-done | bytes 131104 | tf_op jit(solution)/shard_map/ppermute | solution.py:347
  47.4 1.5 %shard_map.100 = (f32[16,32,256]{2,1,0:T(8,128)S(1)}, f32[1024,128]{1,0:T(8,128)}) custom-call(f32[9,32,256]{2,1,0:T(8,128)S(1)} %get-tuple-element.20.own_ref, f32[9,32,256]{2,1,0:T(8,128)S(1)} %collective-permute-done.left_ref, f32[9,32,256]{2,1,0:T(8,128)S(1)} %collective-permute-done.2.right_ref, f32[9,32,256]{2,1,0:T(8,128)S(1)} %collective-permute-done.6.other_ref, ...), custom_call_target="tpu_custom_call" | custom-call | tf_op jit(solution)/shard_map/pallas_call | solution.py:290
  48.9 10.2 %all-to-all-start = ((f32[128,8,128]{2,1,0:T(8,128)}), f32[128,8,128]{2,1,0:T(8,128)S(1)}, u32[]{:S(2)}, u32[]{:S(2)}) async-start(f32[128,8,128]{2,1,0:T(8,128)} %bitcast.1), calls=%async_computation | async-start | bytes 1048576 | tf_op jit(solution)/shard_map/all_to_all | solution.py:300
  59.0 0.2 green.1.green_ref
  59.2 13.9 %all-to-all-done = f32[128,8,128]{2,1,0:T(8,128)S(1)} async-done(((f32[128,8,128]{2,1,0:T(8,128)}), f32[128,8,128]{2,1,0:T(8,128)S(1)}, u32[]{:S(2)}, u32[]{:S(2)}) %all-to-all-start) | async-done | bytes 524320 | tf_op jit(solution)/shard_map/all_to_all | solution.py:300
  73.1 4.5 %shard_map.101 = f32[1024,128]{1,0:T(8,128)} custom-call(f32[2,256,256]{2,1,0:T(8,128)S(1)} %green.1.green_ref, f32[1024,128]{1,0:T(8,128)S(1)} %bitcast.11, bf16[512,256]{1,0:T(8,128)(2,1)S(1)} %copy-done, bf16[512,256]{1,0:T(8,128)(2,1)S(1)} %copy-done.1), custom_call_target="tpu_custom_call" | custom-call | tf_op jit(solution)/shard_map/pallas_call | solution.py:290
  77.7 3.9 %all-to-all-start.1 = ((f32[128,8,128]{2,1,0:T(8,128)}), f32[128,8,128]{2,1,0:T(8,128)S(1)}, u32[]{:S(2)}, u32[]{:S(2)}) async-start(f32[128,8,128]{2,1,0:T(8,128)} %bitcast.3), calls=%async_computation.1 | async-start | bytes 1048576 | tf_op jit(solution)/shard_map/all_to_all | solution.py:300
  81.6 0.8 copy.10
  82.4 13.3 %all-to-all-done.1 = f32[128,8,128]{2,1,0:T(8,128)S(1)} async-done(((f32[128,8,128]{2,1,0:T(8,128)}), f32[128,8,128]{2,1,0:T(8,128)S(1)}, u32[]{:S(2)}, u32[]{:S(2)}) %all-to-all-start.1) | async-done | bytes 524320 | tf_op jit(solution)/shard_map/all_to_all | solution.py:300
  95.7 1.2 %shard_map.102 = f32[16,32,256]{2,1,0:T(8,128)} custom-call(f32[1024,128]{1,0:T(8,128)S(1)} %bitcast.10, bf16[256,256]{1,0:T(8,128)(2,1)S(1)} %copy-done.2, bf16[256,256]{1,0:T(8,128)(2,1)S(1)} %copy-done.3), custom_call_target="tpu_custom_call" | custom-call | tf_op jit(solution)/shard_map/pallas_call | solution.py:290
  (24 shorter events, 0.2 us)
Async XLA Ops:
  2.3 11.4 %collective-permute-start.4 = (f32[9,32,256]{2,1,0:T(8,128)S(1)}, f32[9,32,256]{2,1,0:T(8,128)S(1)}, u32[]{:S(2)}, u32[]{:S(2)}) collective-permute-start(f32[9,32,256]{2,1,0:T(8,128)S(1)} %get-tuple-element.27), channel_id=1, source_target_pairs={{0,48},{1,49},{2,50},{3,51},{4,52},{5,53},{6,54},{7,55},{8,56},{9,... | collective-permute-start | bytes 884744 | tf_op jit(solution)/shard_map/ppermute | solution.py:347
  5.7 13.5 %collective-permute-start.8 = (f32[2,7,32,256]{3,2,1,0:T(8,128)S(1)}, f32[2,7,32,256]{3,2,1,0:T(8,128)S(1)}, u32[]{:S(2)}, u32[]{:S(2)}) collective-permute-start(f32[2,7,32,256]{3,2,1,0:T(8,128)S(1)} %get-tuple-element.31), channel_id=1, source_target_pairs={{0,64},{1,65},{2,66},{3,67},{4,68},{5,69},{6,70},{7,71},{8,72},{9,... | collective-permute-start | bytes 1376264 | tf_op jit(solution)/shard_map/ppermute | solution.py:347
  11.0 36.4 %copy-start.4 = (bf16[256,256]{1,0:T(8,128)(2,1)S(1)}, bf16[256,256]{1,0:T(8,128)(2,1)}, u32[]{:S(2)}) copy-start(bf16[256,256]{1,0:T(8,128)(2,1)} %constant.12.clone.high_ref) | copy-start | bytes 393220
  11.0 36.4 %copy-start.5 = (bf16[256,256]{1,0:T(8,128)(2,1)S(1)}, bf16[256,256]{1,0:T(8,128)(2,1)}, u32[]{:S(2)}) copy-start(bf16[256,256]{1,0:T(8,128)(2,1)} %constant.13.clone.low_ref) | copy-start | bytes 393220
  11.0 18.1 %collective-permute-start.7 = (f32[2,7,32,256]{3,2,1,0:T(8,128)S(1)}, f32[2,7,32,256]{3,2,1,0:T(8,128)S(1)}, u32[]{:S(2)}, u32[]{:S(2)}) collective-permute-start(f32[2,7,32,256]{3,2,1,0:T(8,128)S(1)} %get-tuple-element.29), channel_id=1, source_target_pairs={{0,64},{1,65},{2,66},{3,67},{4,68},{5,69},{6,70},{7,71},{8,72},{9,... | collective-permute-start | bytes 1376264 | tf_op jit(solution)/shard_map/ppermute | solution.py:347
  11.1 8.8 %collective-permute-start.1 = (f32[9,32,256]{2,1,0:T(8,128)S(1)}, f32[9,32,256]{2,1,0:T(8,128)S(1)}, u32[]{:S(2)}, u32[]{:S(2)}) collective-permute-start(f32[9,32,256]{2,1,0:T(8,128)S(1)} %get-tuple-element.23), channel_id=1, source_target_pairs={{0,16},{1,17},{2,18},{3,19},{4,20},{5,21},{6,22},{7,23},{8,24},{9,... | collective-permute-start | bytes 884744 | tf_op jit(solution)/shard_map/ppermute | solution.py:347
  11.2 61.9 %copy-start = (bf16[512,256]{1,0:T(8,128)(2,1)S(1)}, bf16[512,256]{1,0:T(8,128)(2,1)}, u32[]{:S(2)}) copy-start(bf16[512,256]{1,0:T(8,128)(2,1)} %constant.14.clone.high_ref) | copy-start | bytes 786436
  11.2 61.9 %copy-start.1 = (bf16[512,256]{1,0:T(8,128)(2,1)S(1)}, bf16[512,256]{1,0:T(8,128)(2,1)}, u32[]{:S(2)}) copy-start(bf16[512,256]{1,0:T(8,128)(2,1)} %constant.15.clone.low_ref) | copy-start | bytes 786436
  11.2 18.1 %collective-permute-start.3 = (f32[9,32,256]{2,1,0:T(8,128)S(1)}, f32[9,32,256]{2,1,0:T(8,128)S(1)}, u32[]{:S(2)}, u32[]{:S(2)}) collective-permute-start(f32[9,32,256]{2,1,0:T(8,128)S(1)} %get-tuple-element.25), channel_id=1, source_target_pairs={{0,16},{1,17},{2,18},{3,19},{4,20},{5,21},{6,22},{7,23},{8,24},{9,... | collective-permute-start | bytes 884744 | tf_op jit(solution)/shard_map/ppermute | solution.py:347
  13.8 81.9 %copy-start.2 = (bf16[256,256]{1,0:T(8,128)(2,1)S(1)}, bf16[256,256]{1,0:T(8,128)(2,1)}, u32[]{:S(2)}) copy-start(bf16[256,256]{1,0:T(8,128)(2,1)} %constant.16.clone.high_ref) | copy-start | bytes 393220
  13.8 81.9 %copy-start.3 = (bf16[256,256]{1,0:T(8,128)(2,1)S(1)}, bf16[256,256]{1,0:T(8,128)(2,1)}, u32[]{:S(2)}) copy-start(bf16[256,256]{1,0:T(8,128)(2,1)} %constant.17.clone.low_ref) | copy-start | bytes 393220
  13.9 18.0 %collective-permute-start.5 = (f32[9,32,256]{2,1,0:T(8,128)S(1)}, f32[9,32,256]{2,1,0:T(8,128)S(1)}, u32[]{:S(2)}, u32[]{:S(2)}) collective-permute-start(f32[9,32,256]{2,1,0:T(8,128)S(1)} %add.20), channel_id=1, source_target_pairs={{0,48},{1,49},{2,50},{3,51},{4,52},{5,53},{6,54},{7,55},{8,56},{9,... | collective-permute-start | bytes 884744 | tf_op jit(solution)/shard_map/ppermute | solution.py:347
  19.3 9.8 %collective-permute-start.9 = (f32[3,32,256]{2,1,0:T(8,128)S(1)}, f32[3,32,256]{2,1,0:T(8,128)S(1)}, u32[]{:S(2)}, u32[]{:S(2)}) collective-permute-start(f32[3,32,256]{2,1,0:T(8,128)S(1)} %get-tuple-element.34), channel_id=1, source_target_pairs={{0,48},{1,49},{2,50},{3,51},{4,52},{5,53},{6,54},{7,55},{8,56},{9,... | collective-permute-start | bytes 294920 | tf_op jit(solution)/shard_map/ppermute | solution.py:347
  19.9 22.4 %collective-permute-start = (f32[9,32,256]{2,1,0:T(8,128)S(1)}, f32[9,32,256]{2,1,0:T(8,128)S(1)}, u32[]{:S(2)}, u32[]{:S(2)}) collective-permute-start(f32[9,32,256]{2,1,0:T(8,128)S(1)} %get-tuple-element.21), channel_id=1, source_target_pairs={{0,48},{1,49},{2,50},{3,51},{4,52},{5,53},{6,54},{7,55},{8,56},{9,... | collective-permute-start | bytes 884744 | tf_op jit(solution)/shard_map/ppermute | solution.py:347
  29.1 13.3 %collective-permute-start.2 = (f32[9,32,256]{2,1,0:T(8,128)S(1)}, f32[9,32,256]{2,1,0:T(8,128)S(1)}, u32[]{:S(2)}, u32[]{:S(2)}) collective-permute-start(f32[9,32,256]{2,1,0:T(8,128)S(1)} %add.18), channel_id=1, source_target_pairs={{0,16},{1,17},{2,18},{3,19},{4,20},{5,21},{6,22},{7,23},{8,24},{9,... | collective-permute-start | bytes 884744 | tf_op jit(solution)/shard_map/ppermute | solution.py:347
  29.1 13.2 %collective-permute-start.11 = (f32[7,32,256]{2,1,0:T(8,128)S(1)}, f32[7,32,256]{2,1,0:T(8,128)S(1)}, u32[]{:S(2)}, u32[]{:S(2)}) collective-permute-start(f32[7,32,256]{2,1,0:T(8,128)S(1)} %get-tuple-element.35), channel_id=1, source_target_pairs={{0,16},{1,17},{2,18},{3,19},{4,20},{5,21},{6,22},{7,23},{8,24},{9,... | collective-permute-start | bytes 688136 | tf_op jit(solution)/shard_map/ppermute | solution.py:347
  29.3 13.1 %collective-permute-start.10 = (f32[7,32,256]{2,1,0:T(8,128)S(1)}, f32[7,32,256]{2,1,0:T(8,128)S(1)}, u32[]{:S(2)}, u32[]{:S(2)}) collective-permute-start(f32[7,32,256]{2,1,0:T(8,128)S(1)} %shard_map.99), channel_id=1, source_target_pairs={{0,48},{1,49},{2,50},{3,51},{4,52},{5,53},{6,54},{7,55},{8,56},{9,... | collective-permute-start | bytes 688136 | tf_op jit(solution)/shard_map/ppermute | solution.py:347
  32.0 15.4 %collective-permute-start.6 = (f32[9,32,256]{2,1,0:T(8,128)S(1)}, f32[9,32,256]{2,1,0:T(8,128)S(1)}, u32[]{:S(2)}, u32[]{:S(2)}) collective-permute-start(f32[9,32,256]{2,1,0:T(8,128)S(1)} %add_add_fusion), channel_id=1, source_target_pairs={{0,64},{1,65},{2,66},{3,67},{4,68},{5,69},{6,70},{7,71},{8,72},{9,... | collective-permute-start | bytes 884744 | tf_op jit(solution)/shard_map/ppermute | solution.py:347
  42.3 5.1 %collective-permute-start.12 = (f32[4,32,256]{2,1,0:T(8,128)S(1)}, f32[4,32,256]{2,1,0:T(8,128)S(1)}, u32[]{:S(2)}, u32[]{:S(2)}) collective-permute-start(f32[4,32,256]{2,1,0:T(8,128)S(1)} %slice_add_fusion), channel_id=1, source_target_pairs={{0,16},{1,17},{2,18},{3,19},{4,20},{5,21},{6,22},{7,23},{8,24},{9,... | collective-permute-start | bytes 393224 | tf_op jit(solution)/shard_map/ppermute | solution.py:347
  48.9 24.2 %all-to-all-start = ((f32[128,8,128]{2,1,0:T(8,128)}), f32[128,8,128]{2,1,0:T(8,128)S(1)}, u32[]{:S(2)}, u32[]{:S(2)}) async-start(f32[128,8,128]{2,1,0:T(8,128)} %bitcast.1), calls=%async_computation | async-start | bytes 1048576 | tf_op jit(solution)/shard_map/all_to_all | solution.py:300
  77.7 18.0 %all-to-all-start.1 = ((f32[128,8,128]{2,1,0:T(8,128)}), f32[128,8,128]{2,1,0:T(8,128)S(1)}, u32[]{:S(2)}, u32[]{:S(2)}) async-start(f32[128,8,128]{2,1,0:T(8,128)} %bitcast.3), calls=%async_computation.1 | async-start | bytes 1048576 | tf_op jit(solution)/shard_map/all_to_all | solution.py:300

commit v2 on v1

--- a/solution.py
+++ b/solution.py
@@ -60,6 +60,13 @@
     return lax.dot_general(
         first, second, (dims, ((), ())), preferred_element_type=jnp.float32
     )
+
+
+def dot3_apart(left, right, dims):
+    def one(a, b):
+        return lax.dot_general(a, b, (dims, ((), ())), preferred_element_type=jnp.float32)
+
+    return one(left[0], right[0]) + (one(left[1], right[0]) + one(left[0], right[1]))
 
 
 plain = ((1,), (0,))
@@ -159,7 +166,7 @@
     operand = split(
         jnp.concatenate([real * green_a, imag * green_a, real * green_b, imag * green_b], axis=1)
     )
-    both = dot3(stacked, operand, plain)
+    both = dot3_apart(stacked, operand, plain)
     by_cos, by_sin = both[:count], both[count:]
     real_a = by_cos[:, :count] - by_sin[:, count : 2 * count]
     imag_a = by_cos[:, count : 2 * count] + by_sin[:, :count]

time: 97.2 us -> 97.2 us (level)
  no operation moved by 1% of the time
where the time goes in v2:
time: 97.2 us; the launch traced here: 96.9 us
  waiting for transfers between devices  51.3 us (53%)
  starting transfers between devices  30.5 us (31%)
  Pallas kernels  13.3 us (14%)
    all_to_all x2, waiting for transfers between devices, exchange(): return lax.all_to_all(message, axes, 0, 0, tiled=True)  27.2 us
    ppermute x13, waiting for transfers between devices, send(): return lax.ppermute(values, axes, ring(dx, dz))  24.1 us
    ppermute x13, starting transfers between devices, send(): return lax.ppermute(values, axes, ring(dx, dz))  16.5 us
    all_to_all x2, starting transfers between devices, exchange(): return lax.all_to_all(message, axes, 0, 0, tiled=True)  14.1 us
    pallas_call x5, Pallas kernels, vmem_call(): pl.pallas_call(kernel, out_shape=out_shape, in_specs=[vmem] * len(placed)...  7.33 us
    pallas_call x3, Pallas kernels, partial_densities(): pl.pallas_call(lambda *refs: density_kernel(pieces, *refs), out_shape=sha...  5.76 us
  transfers between devices with their start and end apart: 15, of which 6 were waited for; matrix products, arithmetic and copies ran while one was open for 1% of the time, Pallas kernels for 4%

profile of v2, /device:TPU:1, one launch (start us, length us, event | category | flops | bytes accessed | tf_op | source)
XLA Modules:
  0.0 96.9 jit_solution(11629871979470966690)
XLA Ops:
  0.6 1.7 %shard_map.97 = (f32[9,32,256]{2,1,0:T(8,128)S(1)}, f32[9,32,256]{2,1,0:T(8,128)S(1)}, f32[2,7,32,256]{3,2,1,0:T(8,128)S(1)}) custom-call(f32[4]{0:T(128)} %refs_0_.5, bf16[4,16,256,256]{3,2,1,0:T(8,128)(2,1)} %refs_1_.5), custom_call_target="tpu_custom_call" | custom-call | tf_op jit(solution)/shard_map/pallas_call | solution.py:280
  2.3 3.4 %collective-permute-start.4 = (f32[9,32,256]{2,1,0:T(8,128)S(1)}, f32[9,32,256]{2,1,0:T(8,128)S(1)}, u32[]{:S(2)}, u32[]{:S(2)}) collective-permute-start(f32[9,32,256]{2,1,0:T(8,128)S(1)} %get-tuple-element.27), channel_id=1, source_target_pairs={{0,48},{1,49},{2,50},{3,51},{4,52},{5,53},{6,54},{7,55},{8,56},{9,... | collective-permute-start | bytes 884744 | tf_op jit(solution)/shard_map/ppermute | solution.py:354
  5.7 3.6 %collective-permute-start.8 = (f32[2,7,32,256]{3,2,1,0:T(8,128)S(1)}, f32[2,7,32,256]{3,2,1,0:T(8,128)S(1)}, u32[]{:S(2)}, u32[]{:S(2)}) collective-permute-start(f32[2,7,32,256]{3,2,1,0:T(8,128)S(1)} %get-tuple-element.31), channel_id=1, source_target_pairs={{0,64},{1,65},{2,66},{3,67},{4,68},{5,69},{6,70},{7,71},{8,72},{9,... | collective-permute-start | bytes 1376264 | tf_op jit(solution)/shard_map/ppermute | solution.py:354
  9.3 1.7 %shard_map.96 = (f32[9,32,256]{2,1,0:T(8,128)S(1)}, f32[9,32,256]{2,1,0:T(8,128)S(1)}, f32[2,7,32,256]{3,2,1,0:T(8,128)S(1)}) custom-call(f32[4]{0:T(128)} %refs_0_.5, bf16[4,16,256,256]{3,2,1,0:T(8,128)(2,1)} %refs_1_.5), custom_call_target="tpu_custom_call" | custom-call | tf_op jit(solution)/shard_map/pallas_call | solution.py:280
  11.0 0.0 copy-start.4
  11.0 0.0 copy-start.5
  11.0 0.1 collective-permute-start.7
  11.1 0.1 collective-permute-start.1
  11.2 0.0 copy-start
  11.2 0.2 collective-permute-start.3
  11.4 2.4 %shard_map.95 = (f32[9,32,256]{2,1,0:T(8,128)S(1)}, f32[9,32,256]{2,1,0:T(8,128)S(1)}, f32[7,32,256]{2,1,0:T(8,128)S(1)}, f32[7,32,256]{2,1,0:T(8,128)S(1)}, f32...) custom-call(f32[4]{0:T(128)} %refs_0_.5, ...), custom_call_target="tpu_custom_call" | custom-call | tf_op jit(solution)/shard_map/pallas_call | solution.py:280
  13.9 2.7 %collective-permute-start.5 = (f32[9,32,256]{2,1,0:T(8,128)S(1)}, f32[9,32,256]{2,1,0:T(8,128)S(1)}, u32[]{:S(2)}, u32[]{:S(2)}) collective-permute-start(f32[9,32,256]{2,1,0:T(8,128)S(1)} %add.20), channel_id=1, source_target_pairs={{0,48},{1,49},{2,50},{3,51},{4,52},{5,53},{6,54},{7,55},{8,56},{9,... | collective-permute-start | bytes 884744 | tf_op jit(solution)/shard_map/ppermute | solution.py:354
  16.6 2.7 %collective-permute-done.8.cross_ref = f32[2,7,32,256]{3,2,1,0:T(8,128)S(1)} collective-permute-done((f32[2,7,32,256]{3,2,1,0:T(8,128)S(1)}, f32[2,7,32,256]{3,2,1,0:T(8,128)S(1)}, u32[]{:S(2)}, u32[]{:S(2)}) %collective-permute-start.8) | collective-permute-done | bytes 458784 | tf_op jit(solution)/shard_map/ppermute | solution.py:354
  19.3 0.6 collective-permute-start.9
  19.9 0.3 collective-permute-start
  20.2 8.9 %collective-permute-done.7.cross_ref = f32[2,7,32,256]{3,2,1,0:T(8,128)S(1)} collective-permute-done((f32[2,7,32,256]{3,2,1,0:T(8,128)S(1)}, f32[2,7,32,256]{3,2,1,0:T(8,128)S(1)}, u32[]{:S(2)}, u32[]{:S(2)}) %collective-permute-start.7) | collective-permute-done | bytes 458784 | tf_op jit(solution)/shard_map/ppermute | solution.py:354
  29.1 0.2 collective-permute-start.11
  29.3 2.6 %collective-permute-start.10 = (f32[7,32,256]{2,1,0:T(8,128)S(1)}, f32[7,32,256]{2,1,0:T(8,128)S(1)}, u32[]{:S(2)}, u32[]{:S(2)}) collective-permute-start(f32[7,32,256]{2,1,0:T(8,128)S(1)} %shard_map.99), channel_id=1, source_target_pairs={{0,48},{1,49},{2,50},{3,51},{4,52},{5,53},{6,54},{7,55},{8,56},{9,... | collective-permute-start | bytes 688136 | tf_op jit(solution)/shard_map/ppermute | solution.py:354
  31.9 0.1 add_add_fusion
  32.0 2.8 %collective-permute-start.6 = (f32[9,32,256]{2,1,0:T(8,128)S(1)}, f32[9,32,256]{2,1,0:T(8,128)S(1)}, u32[]{:S(2)}, u32[]{:S(2)}) collective-permute-start(f32[9,32,256]{2,1,0:T(8,128)S(1)} %add_add_fusion), channel_id=1, source_target_pairs={{0,64},{1,65},{2,66},{3,67},{4,68},{5,69},{6,70},{7,71},{8,72},{9,... | collective-permute-start | bytes 884744 | tf_op jit(solution)/shard_map/ppermute | solution.py:354
  34.7 7.5 %collective-permute-done.11.ahead_ref = f32[7,32,256]{2,1,0:T(8,128)S(1)} collective-permute-done((f32[7,32,256]{2,1,0:T(8,128)S(1)}, f32[7,32,256]{2,1,0:T(8,128)S(1)}, u32[]{:S(2)}, u32[]{:S(2)}) %collective-permute-start.11) | collective-permute-done | bytes 229408 | tf_op jit(solution)/shard_map/ppermute | solution.py:354
  42.3 0.1 collective-permute-start.12
  42.4 5.0 %collective-permute-done.12.lines1_ref = f32[4,32,256]{2,1,0:T(8,128)S(1)} collective-permute-done((f32[4,32,256]{2,1,0:T(8,128)S(1)}, f32[4,32,256]{2,1,0:T(8,128)S(1)}, u32[]{:S(2)}, u32[]{:S(2)}) %collective-permute-start.12) | collective-permute-done | bytes 131104 | tf_op jit(solution)/shard_map/ppermute | solution.py:354
  47.4 1.5 %shard_map.100 = (f32[16,32,256]{2,1,0:T(8,128)S(1)}, f32[1024,128]{1,0:T(8,128)}) custom-call(f32[9,32,256]{2,1,0:T(8,128)S(1)} %get-tuple-element.20.own_ref, f32[9,32,256]{2,1,0:T(8,128)S(1)} %collective-permute-done.left_ref, f32[9,32,256]{2,1,0:T(8,128)S(1)} %collective-permute-done.2.right_ref, f32[9,32,256]{2,1,0:T(8,128)S(1)} %collective-permute-done.6.other_ref, ...), custom_call_target="tpu_custom_call" | custom-call | tf_op jit(solution)/shard_map/pallas_call | solution.py:297
  48.9 10.2 %all-to-all-start = ((f32[128,8,128]{2,1,0:T(8,128)}), f32[128,8,128]{2,1,0:T(8,128)S(1)}, u32[]{:S(2)}, u32[]{:S(2)}) async-start(f32[128,8,128]{2,1,0:T(8,128)} %bitcast.1), calls=%async_computation | async-start | bytes 1048576 | tf_op jit(solution)/shard_map/all_to_all | solution.py:307
  59.0 0.2 green.1.green_ref
  59.2 13.9 %all-to-all-done = f32[128,8,128]{2,1,0:T(8,128)S(1)} async-done(((f32[128,8,128]{2,1,0:T(8,128)}), f32[128,8,128]{2,1,0:T(8,128)S(1)}, u32[]{:S(2)}, u32[]{:S(2)}) %all-to-all-start) | async-done | bytes 524320 | tf_op jit(solution)/shard_map/all_to_all | solution.py:307
  73.1 4.5 %shard_map.101 = f32[1024,128]{1,0:T(8,128)} custom-call(f32[2,256,256]{2,1,0:T(8,128)S(1)} %green.1.green_ref, f32[1024,128]{1,0:T(8,128)S(1)} %bitcast.11, bf16[512,256]{1,0:T(8,128)(2,1)S(1)} %copy-done, bf16[512,256]{1,0:T(8,128)(2,1)S(1)} %copy-done.1), custom_call_target="tpu_custom_call" | custom-call | tf_op jit(solution)/shard_map/pallas_call | solution.py:297
  77.7 3.9 %all-to-all-start.1 = ((f32[128,8,128]{2,1,0:T(8,128)}), f32[128,8,128]{2,1,0:T(8,128)S(1)}, u32[]{:S(2)}, u32[]{:S(2)}) async-start(f32[128,8,128]{2,1,0:T(8,128)} %bitcast.3), calls=%async_computation.1 | async-start | bytes 1048576 | tf_op jit(solution)/shard_map/all_to_all | solution.py:307
  81.6 0.8 copy.10
  82.4 13.3 %all-to-all-done.1 = f32[128,8,128]{2,1,0:T(8,128)S(1)} async-done(((f32[128,8,128]{2,1,0:T(8,128)}), f32[128,8,128]{2,1,0:T(8,128)S(1)}, u32[]{:S(2)}, u32[]{:S(2)}) %all-to-all-start.1) | async-done | bytes 524320 | tf_op jit(solution)/shard_map/all_to_all | solution.py:307
  95.7 1.2 %shard_map.102 = f32[16,32,256]{2,1,0:T(8,128)} custom-call(f32[1024,128]{1,0:T(8,128)S(1)} %bitcast.10, bf16[256,256]{1,0:T(8,128)(2,1)S(1)} %copy-done.2, bf16[256,256]{1,0:T(8,128)(2,1)S(1)} %copy-done.3), custom_call_target="tpu_custom_call" | custom-call | tf_op jit(solution)/shard_map/pallas_call | solution.py:297
  (24 shorter events, 0.2 us)
Async XLA Ops:
  2.3 11.4 %collective-permute-start.4 = (f32[9,32,256]{2,1,0:T(8,128)S(1)}, f32[9,32,256]{2,1,0:T(8,128)S(1)}, u32[]{:S(2)}, u32[]{:S(2)}) collective-permute-start(f32[9,32,256]{2,1,0:T(8,128)S(1)} %get-tuple-element.27), channel_id=1, source_target_pairs={{0,48},{1,49},{2,50},{3,51},{4,52},{5,53},{6,54},{7,55},{8,56},{9,... | collective-permute-start | bytes 884744 | tf_op jit(solution)/shard_map/ppermute | solution.py:354
  5.7 13.5 %collective-permute-start.8 = (f32[2,7,32,256]{3,2,1,0:T(8,128)S(1)}, f32[2,7,32,256]{3,2,1,0:T(8,128)S(1)}, u32[]{:S(2)}, u32[]{:S(2)}) collective-permute-start(f32[2,7,32,256]{3,2,1,0:T(8,128)S(1)} %get-tuple-element.31), channel_id=1, source_target_pairs={{0,64},{1,65},{2,66},{3,67},{4,68},{5,69},{6,70},{7,71},{8,72},{9,... | collective-permute-start | bytes 1376264 | tf_op jit(solution)/shard_map/ppermute | solution.py:354
  11.0 36.4 %copy-start.4 = (bf16[256,256]{1,0:T(8,128)(2,1)S(1)}, bf16[256,256]{1,0:T(8,128)(2,1)}, u32[]{:S(2)}) copy-start(bf16[256,256]{1,0:T(8,128)(2,1)} %constant.12.clone.high_ref) | copy-start | bytes 393220
  11.0 36.4 %copy-start.5 = (bf16[256,256]{1,0:T(8,128)(2,1)S(1)}, bf16[256,256]{1,0:T(8,128)(2,1)}, u32[]{:S(2)}) copy-start(bf16[256,256]{1,0:T(8,128)(2,1)} %constant.13.clone.low_ref) | copy-start | bytes 393220
  11.0 18.1 %collective-permute-start.7 = (f32[2,7,32,256]{3,2,1,0:T(8,128)S(1)}, f32[2,7,32,256]{3,2,1,0:T(8,128)S(1)}, u32[]{:S(2)}, u32[]{:S(2)}) collective-permute-start(f32[2,7,32,256]{3,2,1,0:T(8,128)S(1)} %get-tuple-element.29), channel_id=1, source_target_pairs={{0,64},{1,65},{2,66},{3,67},{4,68},{5,69},{6,70},{7,71},{8,72},{9,... | collective-permute-start | bytes 1376264 | tf_op jit(solution)/shard_map/ppermute | solution.py:354
  11.1 8.8 %collective-permute-start.1 = (f32[9,32,256]{2,1,0:T(8,128)S(1)}, f32[9,32,256]{2,1,0:T(8,128)S(1)}, u32[]{:S(2)}, u32[]{:S(2)}) collective-permute-start(f32[9,32,256]{2,1,0:T(8,128)S(1)} %get-tuple-element.23), channel_id=1, source_target_pairs={{0,16},{1,17},{2,18},{3,19},{4,20},{5,21},{6,22},{7,23},{8,24},{9,... | collective-permute-start | bytes 884744 | tf_op jit(solution)/shard_map/ppermute | solution.py:354
  11.2 61.9 %copy-start = (bf16[512,256]{1,0:T(8,128)(2,1)S(1)}, bf16[512,256]{1,0:T(8,128)(2,1)}, u32[]{:S(2)}) copy-start(bf16[512,256]{1,0:T(8,128)(2,1)} %constant.14.clone.high_ref) | copy-start | bytes 786436
  11.2 61.9 %copy-start.1 = (bf16[512,256]{1,0:T(8,128)(2,1)S(1)}, bf16[512,256]{1,0:T(8,128)(2,1)}, u32[]{:S(2)}) copy-start(bf16[512,256]{1,0:T(8,128)(2,1)} %constant.15.clone.low_ref) | copy-start | bytes 786436
  11.2 18.1 %collective-permute-start.3 = (f32[9,32,256]{2,1,0:T(8,128)S(1)}, f32[9,32,256]{2,1,0:T(8,128)S(1)}, u32[]{:S(2)}, u32[]{:S(2)}) collective-permute-start(f32[9,32,256]{2,1,0:T(8,128)S(1)} %get-tuple-element.25), channel_id=1, source_target_pairs={{0,16},{1,17},{2,18},{3,19},{4,20},{5,21},{6,22},{7,23},{8,24},{9,... | collective-permute-start | bytes 884744 | tf_op jit(solution)/shard_map/ppermute | solution.py:354
  13.8 81.9 %copy-start.2 = (bf16[256,256]{1,0:T(8,128)(2,1)S(1)}, bf16[256,256]{1,0:T(8,128)(2,1)}, u32[]{:S(2)}) copy-start(bf16[256,256]{1,0:T(8,128)(2,1)} %constant.16.clone.high_ref) | copy-start | bytes 393220
  13.8 81.9 %copy-start.3 = (bf16[256,256]{1,0:T(8,128)(2,1)S(1)}, bf16[256,256]{1,0:T(8,128)(2,1)}, u32[]{:S(2)}) copy-start(bf16[256,256]{1,0:T(8,128)(2,1)} %constant.17.clone.low_ref) | copy-start | bytes 393220
  13.9 18.0 %collective-permute-start.5 = (f32[9,32,256]{2,1,0:T(8,128)S(1)}, f32[9,32,256]{2,1,0:T(8,128)S(1)}, u32[]{:S(2)}, u32[]{:S(2)}) collective-permute-start(f32[9,32,256]{2,1,0:T(8,128)S(1)} %add.20), channel_id=1, source_target_pairs={{0,48},{1,49},{2,50},{3,51},{4,52},{5,53},{6,54},{7,55},{8,56},{9,... | collective-permute-start | bytes 884744 | tf_op jit(solution)/shard_map/ppermute | solution.py:354
  19.3 9.8 %collective-permute-start.9 = (f32[3,32,256]{2,1,0:T(8,128)S(1)}, f32[3,32,256]{2,1,0:T(8,128)S(1)}, u32[]{:S(2)}, u32[]{:S(2)}) collective-permute-start(f32[3,32,256]{2,1,0:T(8,128)S(1)} %get-tuple-element.34), channel_id=1, source_target_pairs={{0,48},{1,49},{2,50},{3,51},{4,52},{5,53},{6,54},{7,55},{8,56},{9,... | collective-permute-start | bytes 294920 | tf_op jit(solution)/shard_map/ppermute | solution.py:354
  19.9 22.4 %collective-permute-start = (f32[9,32,256]{2,1,0:T(8,128)S(1)}, f32[9,32,256]{2,1,0:T(8,128)S(1)}, u32[]{:S(2)}, u32[]{:S(2)}) collective-permute-start(f32[9,32,256]{2,1,0:T(8,128)S(1)} %get-tuple-element.21), channel_id=1, source_target_pairs={{0,48},{1,49},{2,50},{3,51},{4,52},{5,53},{6,54},{7,55},{8,56},{9,... | collective-permute-start | bytes 884744 | tf_op jit(solution)/shard_map/ppermute | solution.py:354
  29.1 13.3 %collective-permute-start.2 = (f32[9,32,256]{2,1,0:T(8,128)S(1)}, f32[9,32,256]{2,1,0:T(8,128)S(1)}, u32[]{:S(2)}, u32[]{:S(2)}) collective-permute-start(f32[9,32,256]{2,1,0:T(8,128)S(1)} %add.18), channel_id=1, source_target_pairs={{0,16},{1,17},{2,18},{3,19},{4,20},{5,21},{6,22},{7,23},{8,24},{9,... | collective-permute-start | bytes 884744 | tf_op jit(solution)/shard_map/ppermute | solution.py:354
  29.1 13.2 %collective-permute-start.11 = (f32[7,32,256]{2,1,0:T(8,128)S(1)}, f32[7,32,256]{2,1,0:T(8,128)S(1)}, u32[]{:S(2)}, u32[]{:S(2)}) collective-permute-start(f32[7,32,256]{2,1,0:T(8,128)S(1)} %get-tuple-element.35), channel_id=1, source_target_pairs={{0,16},{1,17},{2,18},{3,19},{4,20},{5,21},{6,22},{7,23},{8,24},{9,... | collective-permute-start | bytes 688136 | tf_op jit(solution)/shard_map/ppermute | solution.py:354
  29.3 13.1 %collective-permute-start.10 = (f32[7,32,256]{2,1,0:T(8,128)S(1)}, f32[7,32,256]{2,1,0:T(8,128)S(1)}, u32[]{:S(2)}, u32[]{:S(2)}) collective-permute-start(f32[7,32,256]{2,1,0:T(8,128)S(1)} %shard_map.99), channel_id=1, source_target_pairs={{0,48},{1,49},{2,50},{3,51},{4,52},{5,53},{6,54},{7,55},{8,56},{9,... | collective-permute-start | bytes 688136 | tf_op jit(solution)/shard_map/ppermute | solution.py:354
  32.0 15.4 %collective-permute-start.6 = (f32[9,32,256]{2,1,0:T(8,128)S(1)}, f32[9,32,256]{2,1,0:T(8,128)S(1)}, u32[]{:S(2)}, u32[]{:S(2)}) collective-permute-start(f32[9,32,256]{2,1,0:T(8,128)S(1)} %add_add_fusion), channel_id=1, source_target_pairs={{0,64},{1,65},{2,66},{3,67},{4,68},{5,69},{6,70},{7,71},{8,72},{9,... | collective-permute-start | bytes 884744 | tf_op jit(solution)/shard_map/ppermute | solution.py:354
  42.3 5.1 %collective-permute-start.12 = (f32[4,32,256]{2,1,0:T(8,128)S(1)}, f32[4,32,256]{2,1,0:T(8,128)S(1)}, u32[]{:S(2)}, u32[]{:S(2)}) collective-permute-start(f32[4,32,256]{2,1,0:T(8,128)S(1)} %slice_add_fusion), channel_id=1, source_target_pairs={{0,16},{1,17},{2,18},{3,19},{4,20},{5,21},{6,22},{7,23},{8,24},{9,... | collective-permute-start | bytes 393224 | tf_op jit(solution)/shard_map/ppermute | solution.py:354
  48.9 24.2 %all-to-all-start = ((f32[128,8,128]{2,1,0:T(8,128)}), f32[128,8,128]{2,1,0:T(8,128)S(1)}, u32[]{:S(2)}, u32[]{:S(2)}) async-start(f32[128,8,128]{2,1,0:T(8,128)} %bitcast.1), calls=%async_computation | async-start | bytes 1048576 | tf_op jit(solution)/shard_map/all_to_all | solution.py:307
  77.7 18.0 %all-to-all-start.1 = ((f32[128,8,128]{2,1,0:T(8,128)}), f32[128,8,128]{2,1,0:T(8,128)S(1)}, u32[]{:S(2)}, u32[]{:S(2)}) async-start(f32[128,8,128]{2,1,0:T(8,128)} %bitcast.3), calls=%async_computation.1 | async-start | bytes 1048576 | tf_op jit(solution)/shard_map/all_to_all | solution.py:307
